TPU v7x, 32 devices: a whole 2x2x4 slice. The times are simulated.
32 devices in a mesh: feat: 16 (over z, y, x), dp: 2 (over core).
Axes of the slice: x: 2, y: 2, z: 4, core: 2. Of those that a mesh axis runs over, the one named last changes fastest.
Arguments:
- activations: bfloat16 [1024, 16384], P('dp', 'feat')
- norm_gain: float32 [16384], replicated, may hold values from 0.5 to 1.5
- weights: float32 [1024, 16384], P('dp', 'feat'), may hold values from -6 to 6
- inverse_factor: float32 [128, 16384], P(None, 'feat'), as said below
- grid_scales: float32 [1024], P('dp'), may hold values from 0.5 to 2
Outputs:
- hessian: float32 [16384, 16384], P('dp', 'feat')
- updated_weights: float32 [1024, 16384], P('dp', 'feat')
Inputs may be any that keep to these rules, and one draw needn't show every extreme that they name: `inverse_factor`: in the first 128 columns, the diagonal lies in 1 to 2 and entries below it are zero.
All inputs are finite; a program needn't handle non-finite values.
Results may differ from a plain program's by a relative error of at most 0.012.
Values may be sent and summed in bfloat16 or wider, within the bound.
No kernel may reach another device: no remote copies, remote signals or barrier semaphores. Data moves between devices by JAX's collectives and lax.ppermute only.
A program may use at most 128 MiB of HBM per device.

v0:
```python
import math
import jax
import jax.numpy as jnp
from jax import lax
from jax.sharding import PartitionSpec as P

norm_epsilon = 1e-05
full_turn = 2.0 * math.pi


def spread(value, axis, source):
    kept = jnp.where(lax.axis_index(axis) == source, value, 0).astype(value.dtype)
    return lax.psum(kept, axis)


def quantize_panel(panel_rows, factor_block, grid_scales):
    panel_width = factor_block.shape[0]
    diagonal_entries = jnp.diagonal(factor_block)
    positions = jnp.arange(panel_width)

    def advance(index, carry):
        working, quantized, residue = carry
        current = lax.dynamic_index_in_dim(working, index, 0, keepdims=False)
        grid_ratio = current / grid_scales
        dequantized = grid_scales * (grid_ratio - jnp.sin(full_turn * grid_ratio) / full_turn)
        pivot_entry = lax.dynamic_index_in_dim(diagonal_entries, index, 0, keepdims=False)
        scaled_error = (current - dequantized) / pivot_entry
        factor_row = lax.dynamic_index_in_dim(factor_block, index, 0, keepdims=False)
        factor_row = jnp.where(positions > index, factor_row, jnp.zeros_like(factor_row))
        working = working - factor_row[:, None] * scaled_error[None, :]
        quantized = lax.dynamic_update_index_in_dim(quantized, dequantized, index, 0)
        residue = lax.dynamic_update_index_in_dim(residue, scaled_error, index, 0)
        return (working, quantized, residue)

    blank = jnp.zeros_like(panel_rows)
    final = lax.fori_loop(0, panel_width, advance, (panel_rows, blank, blank))
    return (final[1], final[2])


def body(activations, norm_gain, weights, inverse_factor, grid_scales):
    shard_width = activations.shape[1]
    row_count = activations.shape[0]
    full_width = shard_width * lax.axis_size("feat")
    token_total = row_count * lax.axis_size("dp")
    own_start = lax.axis_index("feat") * shard_width
    own_gain = lax.dynamic_slice_in_dim(norm_gain, own_start, shard_width, 0)
    widened = activations.astype(jnp.float32)
    own_squares = jnp.sum(widened * widened, axis=1, keepdims=True)
    row_squares = lax.psum(own_squares, "feat")
    normed = (
        widened * lax.rsqrt(row_squares / full_width + norm_epsilon) * own_gain[None, :]
    ).astype(jnp.bfloat16)
    gathered = lax.all_gather(normed, "feat", axis=1, tiled=True)
    product = lax.dot_general(
        gathered, normed, (((0,), (0,)), ((), ())), preferred_element_type=jnp.float32
    )
    hessian = lax.psum_scatter(
        (product / token_total).astype(jnp.bfloat16), "dp", scatter_dimension=0, tiled=True
    ).astype(jnp.float32)
    panel_width = inverse_factor.shape[0]
    quantized, residue = quantize_panel(
        weights[:, :panel_width].T, inverse_factor[:, :panel_width], grid_scales
    )
    residue = spread(residue.astype(jnp.bfloat16), "feat", 0).astype(residue.dtype)
    shift_terms = lax.dot_general(
        residue,
        inverse_factor,
        (((0,), (0,)), ((), ())),
        precision=lax.Precision.HIGHEST,
        preferred_element_type=jnp.float32,
    )
    updated = weights - shift_terms
    column_ids = lax.broadcasted_iota(jnp.int32, weights.shape, 1)
    panel_mask = (column_ids < panel_width) & (lax.axis_index("feat") == 0)
    padded_panel = jnp.pad(quantized.T, ((0, 0), (0, shard_width - panel_width)))
    updated = jnp.where(panel_mask, padded_panel, updated)
    return (hessian, updated)


def solution(mesh):
    placed = (P("dp", "feat"), P(), P("dp", "feat"), P(None, "feat"), P("dp"))
    return jax.shard_map(
        body,
        mesh=mesh,
        in_specs=placed,
        out_specs=(P("dp", "feat"), P("dp", "feat")),
        check_vma=False,
    )
```

profile of v0, /device:TPU:0, one launch (start us, length us, event | category | flops | bytes accessed | tf_op | source)
XLA Modules:
  0.0 446.7 jit_solution(7831855614738528062)
XLA Ops:
  7.2 1.6 fusion.2
  8.8 43.6 %psum.14 = f32[512,1]{0,1:T(1,128)S(1)} all-reduce(f32[512,1]{0,1:T(1,128)S(1)} %bitcast.28), channel_id=1, replica_groups=mesh['feat'=16,'dp'=2] {'feat'}, use_global_device_ids=true, to_apply=%region_1.0 | all-reduce | flops 512 | bytes 4096 | tf_op jit(solution)/shard_map/psum | solution.py:49
  53.2 2.5 fusion.4
  56.0 1.2 gather_fusion
  57.2 217.8 %while.18 = (s32[]{:T(128)}, f32[128,512]{1,0:T(8,128)S(1)}, f32[128,512]{1,0:T(8,128)S(1)}, bf16[128,512]{1,0:T(8,128)(2,1)S(1)}, f32[128,128]{1,0:T(8,128)S(1)...) while((s32[]{:T(128)}, f32[128,512]{1,0:T(8,128)S(1)}, ...), condition=%wide.region_4.5_spmd.clone, body=%wide.region_3.4_spmd.clone.sunk | while | flops 134914 | bytes 545401 | solution.py:36
  57.9 0.8 subtract_divide_fusion.2
  59.6 0.8 subtract_divide_fusion.2
  63.0 0.8 subtract_divide_fusion.2
  64.7 0.8 subtract_divide_fusion.2
  66.4 0.8 subtract_divide_fusion.2
  68.1 0.8 subtract_divide_fusion.2
  80.0 0.8 subtract_divide_fusion.2
  88.5 0.8 subtract_divide_fusion.2
  139.6 0.8 subtract_divide_fusion.2
  143.0 0.8 subtract_divide_fusion.2
  146.4 0.8 subtract_divide_fusion.2
  168.5 0.8 subtract_divide_fusion.2
  170.2 0.8 subtract_divide_fusion.2
  180.4 0.8 subtract_divide_fusion.2
  275.8 27.8 %multiply_convert_fusion = bf16[16384,1024]{1,0:T(8,128)(2,1)} fusion(bf16[512,16384]{1,0:T(8,128)(2,1)} %all-gather.2.cloned.1.call-done, bf16[512,1024]{1,0:T(8,128)(2,1)S(1)} %copy-done), kind=kOutput, calls=%fused_computation.6 | convolution fusion | flops 17213423616 | bytes 51380224 | tf_op jit(solution)/shard_map/dot_general | solution.py:54
  303.8 73.4 %all-reduce.3.cloned.1.call-done = bf16[128,512]{1,0:T(8,128)(2,1)} async-done(((bf16[128,512]{1,0:T(8,128)(2,1)}), bf16[128,512]{1,0:T(8,128)(2,1)}) %all-reduce.3.cloned.1.call-update) | async-done | bytes 131088 | tf_op jit(solution)/shard_map/psum | solution.py:13
  377.2 3.3 subtract_select_fusion
  380.5 41.1 %reduce-scatter.2.cloned.1.call-done = bf16[8192,1024]{1,0:T(8,128)(2,1)} async-done(((bf16[16384,1024]{1,0:T(8,128)(2,1)}), bf16[8192,1024]{1,0:T(8,128)(2,1)}) %reduce-scatter.2.cloned.1.call-update) | async-done | bytes 16777232 | tf_op jit(solution)/shard_map/reduce_scatter | solution.py:57
  421.6 18.6 %convert_element_type.23 = f32[8192,1024]{1,0:T(8,128)} convert(bf16[8192,1024]{1,0:T(8,128)(2,1)} %reduce-scatter.2.cloned.1.call-done) | non-fusion elementwise | flops 8388608 | bytes 50331648 | tf_op jit(solution)/shard_map/convert_element_type | solution.py:59
  (781 shorter events, 202.9 us)
Async XLA Ops:
  7.2 268.6 %all-gather.2.cloned.1.call-start = ((), (), s32[]{:S(2)}) async-start(), calls=%async_computation.1 | async-start | bytes 17825792 | tf_op jit(solution)/shard_map/all_gather | solution.py:53
  7.2 48.6 %copy-start.2 = (f32[128,1024]{1,0:T(8,128)S(1)}, f32[128,1024]{1,0:T(8,128)}, u32[]{:S(2)}) copy-start(f32[128,1024]{1,0:T(8,128)} %param.10) | copy-start | bytes 1572868
  8.8 47.0 %slice-start = ((f32[512,1024]{1,0:T(8,128)}), f32[512,128]{1,0:T(8,128)S(1)}, s32[]{:S(2)}) async-start(f32[512,1024]{1,0:T(8,128)} %param.9), calls=%async_computation.4 | async-start | bytes 524288 | tf_op jit(solution)/shard_map/slice | solution.py:62
  53.1 4.1 copy-start.3
  55.7 321.5 %all-reduce.3.cloned.1.call-start = ((), (), s32[]{:S(2)}) async-start(), calls=%async_computation.3 | async-start | bytes 262144 | tf_op jit(solution)/shard_map/psum | solution.py:13
  55.9 219.9 %copy-start = (bf16[512,1024]{1,0:T(8,128)(2,1)S(1)}, bf16[512,1024]{1,0:T(8,128)(2,1)}, u32[]{:S(2)}) copy-start(bf16[512,1024]{1,0:T(8,128)(2,1)} %fusion.4) | copy-start | bytes 3145732
  275.7 145.8 %reduce-scatter.2.cloned.1.call-start = ((), (), s32[]{:S(2)}) async-start(), calls=%async_computation.2 | async-start | bytes 50331648 | tf_op jit(solution)/shard_map/reduce_scatter | solution.py:57
  303.6 73.6 %copy-start.1 = (f32[512,1024]{1,0:T(8,128)S(1)}, f32[512,1024]{1,0:T(8,128)}, u32[]{:S(2)}) copy-start(f32[512,1024]{1,0:T(8,128)} %param.9) | copy-start | bytes 6291460
Sparse Core Ops, SparseCore 0:
  55.8 191.9 all-gather.1
  275.9 101.2 all-reduce.2
  380.0 41.4 reduce-scatter.1
where the time goes:
time: 448 us; the launch traced here: 447 us
  other arithmetic  137 us (31%)
  waiting for transfers between devices  115 us (26%)
  local copies, waits for them, and re-layouts  101 us (23%)
  blocking collectives  43.6 us (10%)
  matrix products  31.1 us (7%)
  between operations  13.9 us (3%)
  loops' own time  5.98 us (1%)
    div x128, other arithmetic, advance(): scaled_error = (current - dequantized) / pivot_entry  98.6 us
    dynamic_slice x128, local copies, waits for them, and re-layouts, advance(): lax.dynamic_index_in_dim(diagonal_entries, index, 0, keepdims=False)  85 us
    psum x1, waiting for transfers between devices, spread(): return lax.psum(kept, axis)  73.4 us
    psum x1, blocking collectives, body(): row_squares = lax.psum(own_squares, 'feat')  43.6 us
    reduce_scatter x1, waiting for transfers between devices, body(): lax.psum_scatter((product / token_total).astype(jnp.bfloat16), 'dp', scat...  41.1 us
    dot_general x1, matrix products, body(): lax.dot_general(gathered, normed, (((0,), (0,)), ((), ())), preferred_ele...  27.8 us
    convert_element_type x1, other arithmetic, body(): hessian = lax.psum_scatter((product / token_total).astype(jnp.bfloat16),...  18.6 us
    sub x128, other arithmetic, advance(): working = working - factor_row[:, None] * scaled_error[None, :]  12.9 us
  transfers between devices with their start and end apart: 3, of which 2 were waited for; matrix products, arithmetic and copies ran while one was open for 55% of the time, Pallas kernels for 0%

commit v1 on v0

--- a/solution.py
+++ b/solution.py
@@ -46,7 +46,7 @@
     own_gain = lax.dynamic_slice_in_dim(norm_gain, own_start, shard_width, 0)
     widened = activations.astype(jnp.float32)
     own_squares = jnp.sum(widened * widened, axis=1, keepdims=True)
-    row_squares = lax.psum(own_squares, "feat")
+    row_squares = jnp.sum(lax.all_gather(own_squares, "feat"), axis=0)
     normed = (
         widened * lax.rsqrt(row_squares / full_width + norm_epsilon) * own_gain[None, :]
     ).astype(jnp.bfloat16)

time: 448 us -> 447 us (level)
    psum x1 -> x0, blocking collectives: 43.6 us -> none  [body(): row_squares = lax.psum(own_squares, 'feat')]
    all_gather x0 -> x1, blocking collectives: none -> 42.7 us  [body(): row_squares = jnp.sum(lax.all_gather(own_squares, 'feat'), axis=0)]
where the time goes in v1:
time: 447 us; the launch traced here: 446 us
  other arithmetic  137 us (31%)
  waiting for transfers between devices  115 us (26%)
  local copies, waits for them, and re-layouts  101 us (23%)
  blocking collectives  42.7 us (10%)
  matrix products  31.1 us (7%)
  between operations  13.9 us (3%)
  loops' own time  5.98 us (1%)
    div x128, other arithmetic, advance(): scaled_error = (current - dequantized) / pivot_entry  98.6 us
    dynamic_slice x128, local copies, waits for them, and re-layouts, advance(): lax.dynamic_index_in_dim(diagonal_entries, index, 0, keepdims=False)  85 us
    psum x1, waiting for transfers between devices, spread(): return lax.psum(kept, axis)  73.4 us
    all_gather x1, blocking collectives, body(): row_squares = jnp.sum(lax.all_gather(own_squares, 'feat'), axis=0)  42.7 us
    reduce_scatter x1, waiting for transfers between devices, body(): lax.psum_scatter((product / token_total).astype(jnp.bfloat16), 'dp', scat...  41.1 us
    dot_general x1, matrix products, body(): lax.dot_general(gathered, normed, (((0,), (0,)), ((), ())), preferred_ele...  27.7 us
    convert_element_type x1, other arithmetic, body(): hessian = lax.psum_scatter((product / token_total).astype(jnp.bfloat16),...  18.6 us
    sub x128, other arithmetic, advance(): working = working - factor_row[:, None] * scaled_error[None, :]  12.9 us
  transfers between devices with their start and end apart: 3, of which 2 were waited for; matrix products, arithmetic and copies ran while one was open for 55% of the time, Pallas kernels for 0%

profile of v1, /device:TPU:0, one launch (start us, length us, event | category | flops | bytes accessed | tf_op | source)
XLA Modules:
  0.0 445.8 jit_solution(2222960148220124596)
XLA Ops:
  7.2 1.6 fusion.2
  8.8 42.7 %all-gather.1 = f32[16,1,512]{2,1,0:T(1,128)S(1)} all-gather(f32[1,1,512]{2,1,0:T(1,128)S(1)} %bitcast.26), channel_id=2, replica_groups=mesh['feat'=16,'dp'=2] {'feat'}, dimensions={0}, use_global_device_ids=true | all-gather | bytes 34816 | tf_op jit(solution)/shard_map/all_gather | solution.py:49
  52.2 2.5 fusion.4
  55.1 1.2 gather_fusion
  56.3 217.8 %while.18 = (s32[]{:T(128)}, f32[128,512]{1,0:T(8,128)S(1)}, f32[128,512]{1,0:T(8,128)S(1)}, bf16[128,512]{1,0:T(8,128)(2,1)S(1)}, f32[128,128]{1,0:T(8,128)S(1)...) while((s32[]{:T(128)}, f32[128,512]{1,0:T(8,128)S(1)}, ...), condition=%wide.region_4.5_spmd.clone, body=%wide.region_3.4_spmd.clone.sunk | while | flops 134914 | bytes 545401 | solution.py:36
  57.0 0.8 subtract_divide_fusion.2
  58.7 0.8 subtract_divide_fusion.2
  60.4 0.8 subtract_divide_fusion.2
  79.1 0.8 subtract_divide_fusion.2
  87.6 0.8 subtract_divide_fusion.2
  89.3 0.8 subtract_divide_fusion.2
  99.5 0.8 subtract_divide_fusion.2
  142.1 0.8 subtract_divide_fusion.2
  143.8 0.8 subtract_divide_fusion.2
  167.6 0.8 subtract_divide_fusion.2
  169.3 0.8 subtract_divide_fusion.2
  171.0 0.8 subtract_divide_fusion.2
  201.6 0.8 subtract_divide_fusion.2
  203.3 0.8 subtract_divide_fusion.2
  274.9 27.7 %multiply_convert_fusion = bf16[16384,1024]{1,0:T(8,128)(2,1)} fusion(bf16[512,16384]{1,0:T(8,128)(2,1)} %all-gather.4.cloned.1.call-done, bf16[512,1024]{1,0:T(8,128)(2,1)S(1)} %copy-done), kind=kOutput, calls=%fused_computation.6 | convolution fusion | flops 17213423616 | bytes 51380224 | tf_op jit(solution)/shard_map/dot_general | solution.py:54
  302.8 73.4 %all-reduce.3.cloned.1.call-done = bf16[128,512]{1,0:T(8,128)(2,1)} async-done(((bf16[128,512]{1,0:T(8,128)(2,1)}), bf16[128,512]{1,0:T(8,128)(2,1)}) %all-reduce.3.cloned.1.call-update) | async-done | bytes 131088 | tf_op jit(solution)/shard_map/psum | solution.py:13
  376.3 3.3 subtract_select_fusion
  379.6 41.1 %reduce-scatter.2.cloned.1.call-done = bf16[8192,1024]{1,0:T(8,128)(2,1)} async-done(((bf16[16384,1024]{1,0:T(8,128)(2,1)}), bf16[8192,1024]{1,0:T(8,128)(2,1)}) %reduce-scatter.2.cloned.1.call-update) | async-done | bytes 16777232 | tf_op jit(solution)/shard_map/reduce_scatter | solution.py:57
  420.7 18.6 %convert_element_type.23 = f32[8192,1024]{1,0:T(8,128)} convert(bf16[8192,1024]{1,0:T(8,128)(2,1)} %reduce-scatter.2.cloned.1.call-done) | non-fusion elementwise | flops 8388608 | bytes 50331648 | tf_op jit(solution)/shard_map/convert_element_type | solution.py:59
  (782 shorter events, 202.9 us)
Async XLA Ops:
  7.2 267.7 %all-gather.4.cloned.1.call-start = ((), (), s32[]{:S(2)}) async-start(), calls=%async_computation.1 | async-start | bytes 17825792 | tf_op jit(solution)/shard_map/all_gather | solution.py:53
  7.2 47.7 %copy-start.2 = (f32[128,1024]{1,0:T(8,128)S(1)}, f32[128,1024]{1,0:T(8,128)}, u32[]{:S(2)}) copy-start(f32[128,1024]{1,0:T(8,128)} %param.10) | copy-start | bytes 1572868
  8.8 46.1 %slice-start = ((f32[512,1024]{1,0:T(8,128)}), f32[512,128]{1,0:T(8,128)S(1)}, s32[]{:S(2)}) async-start(f32[512,1024]{1,0:T(8,128)} %param.9), calls=%async_computation.4 | async-start | bytes 524288 | tf_op jit(solution)/shard_map/slice | solution.py:62
  52.2 4.1 copy-start.3
  54.8 321.5 %all-reduce.3.cloned.1.call-start = ((), (), s32[]{:S(2)}) async-start(), calls=%async_computation.3 | async-start | bytes 262144 | tf_op jit(solution)/shard_map/psum | solution.py:13
  55.0 219.9 %copy-start = (bf16[512,1024]{1,0:T(8,128)(2,1)S(1)}, bf16[512,1024]{1,0:T(8,128)(2,1)}, u32[]{:S(2)}) copy-start(bf16[512,1024]{1,0:T(8,128)(2,1)} %fusion.4) | copy-start | bytes 3145732
  274.8 145.8 %reduce-scatter.2.cloned.1.call-start = ((), (), s32[]{:S(2)}) async-start(), calls=%async_computation.2 | async-start | bytes 50331648 | tf_op jit(solution)/shard_map/reduce_scatter | solution.py:57
  302.7 73.6 %copy-start.1 = (f32[512,1024]{1,0:T(8,128)S(1)}, f32[512,1024]{1,0:T(8,128)}, u32[]{:S(2)}) copy-start(f32[512,1024]{1,0:T(8,128)} %param.9) | copy-start | bytes 6291460
Sparse Core Ops, SparseCore 0:
  54.9 192.1 all-gather.3
  275.0 101.2 all-reduce.2
  379.1 41.4 reduce-scatter.1
